TPU v7x, 32 devices: a whole 2x2x4 slice. The times are simulated.
32 devices in a mesh: groups: 2 (over y), markov: 4 (over z), storage: 2 (over x), sub: 2 (over core).
Axes of the slice: x: 2, y: 2, z: 4, core: 2. Of those that a mesh axis runs over, the one named last changes fastest.
Arguments:
- expected_cot: bfloat16 [8192, 2048], P(('groups', 'markov'), ('storage', 'sub')), parts along dimension 0, may hold values from -192 to 192
- value_next: bfloat16 [8192, 2048], P(('groups', 'markov'), ('storage', 'sub')), parts along dimension 0, may hold values from -0.0024414062 to 0.0024414062
- transition: bfloat16 [8192, 4096], P(('groups', 'storage', 'sub'), 'markov'), parts along dimension 0, may hold values from 6.1035156e-05 to 0.0009765625
- section: int32 [2], P('groups'), parts along dimension 0, may hold values from 0 to 51
Outputs:
- section_adjoint: float32 [8192, 2048], P(('groups', 'markov'), ('storage', 'sub')), parts along dimension 0
- transition_grad: float32 [8192, 4096], P(('groups', 'storage', 'sub'), 'markov'), parts along dimension 0
There are 2 independent parts, one for each index of `groups`. A program takes and returns all parts, laid end to end along the dimension named above; each array names one. Nothing has to cross between parts.
All inputs are finite; a program needn't handle non-finite values.
Results may differ from a plain program's by a relative error of at most 0.0003.
Values may be sent and summed in bfloat16 or wider, within the bound.
A program may use at most 64 MiB of HBM per device.

v0:
```python
import jax
import jax.numpy as jnp
from jax import lax
from jax.sharding import PartitionSpec as P

discount_rate = 0.97


def shards(expected_cot, value_next, transition, section):
    discount_factor = jnp.exp(section[0].astype(jnp.float32) * jnp.log(jnp.float32(discount_rate)))
    cotangent_all = lax.all_gather(expected_cot, "markov", axis=0, tiled=True)
    adjoint_sum = lax.dot_general(
        lax.all_gather(transition, ("storage", "sub"), axis=0, tiled=True),
        cotangent_all,
        (((0,), (0,)), ((), ())),
        preferred_element_type=jnp.float32,
    )
    own_states = lax.all_to_all(
        cotangent_all, ("storage", "sub"), split_axis=0, concat_axis=1, tiled=True
    )
    gathered_values = lax.all_gather(value_next, ("storage", "sub"), axis=1, tiled=True)
    gradient_sum = lax.dot_general(
        own_states, gathered_values, (((1,), (1,)), ((), ())), preferred_element_type=jnp.float32
    )
    return (discount_factor * adjoint_sum, discount_factor * gradient_sum)


def solution(mesh):
    return jax.shard_map(
        shards,
        mesh=mesh,
        in_specs=(
            P(("groups", "markov"), ("storage", "sub")),
            P(("groups", "markov"), ("storage", "sub")),
            P(("groups", "storage", "sub"), "markov"),
            P("groups"),
        ),
        out_specs=(
            P(("groups", "markov"), ("storage", "sub")),
            P(("groups", "storage", "sub"), "markov"),
        ),
        check_vma=False,
    )
```

profile of v0, /device:TPU:0, one launch (start us, length us, event | category | flops | bytes accessed | tf_op | source)
XLA Modules:
  0.0 232.1 jit_solution(16197326605313307399)
XLA Ops:
  7.2 0.0 all-gather.6.cloned.1.call-start
  7.2 0.7 all-gather.6.cloned.1.call-update
  7.9 0.0 all-gather.8.cloned.1.call-start
  7.9 0.7 all-gather.8.cloned.1.call-update
  8.6 0.0 all-gather.4.cloned.1.call-start
  8.7 0.7 all-gather.4.cloned.1.call-update
  9.4 83.7 %all-gather.6.cloned.1.call-done = bf16[4096,512]{1,0:T(8,128)(2,1)} async-done(((bf16[1024,512]{1,0:T(8,128)(2,1)}), bf16[4096,512]{1,0:T(8,128)(2,1)}) %all-gather.6.cloned.1.call-update) | async-done | bytes 4194320 | tf_op jit(solution)/shard_map/all_gather | solution.py:11
  93.0 4.9 %all-to-all-start = ((bf16[4,1024,512]{2,1,0:T(8,128)(2,1)}), bf16[4,1024,512]{2,1,0:T(8,128)(2,1)}, u32[]{:S(2)}, u32[]{:S(2)}) async-start(bf16[4,1024,512]{2,1,0:T(8,128)(2,1)} %bitcast.8), calls=%async_computation | async-start | bytes 8388608 | tf_op jit(solution)/shard_map/all_to_all | solution.py:18
  98.6 75.7 %all-to-all-done = bf16[4,1024,512]{2,1,0:T(8,128)(2,1)} async-done(((bf16[4,1024,512]{2,1,0:T(8,128)(2,1)}), bf16[4,1024,512]{2,1,0:T(8,128)(2,1)}, u32[]{:S(2)}, u32[]{:S(2)}) %all-to-all-start) | async-done | bytes 4194336 | tf_op jit(solution)/shard_map/all_to_all | solution.py:18
  174.3 6.3 %copy.6 = bf16[1024,4,512]{0,2,1:T(8,128)(2,1)} copy(bf16[1024,4,512]{2,0,1:T(8,128)(2,1)} %bitcast.2) | data formatting | bytes 8388608 | tf_op jit(solution)/shard_map/all_to_all | solution.py:18
  180.6 0.0 all-gather.8.cloned.1.call-done
  180.6 10.0 %convolution_multiply_fusion = f32[1024,1024]{1,0:T(8,128)} fusion(bf16[1024,2048]{0,1:T(8,128)(2,1)} %bitcast.9, bf16[1024,2048]{1,0:T(8,128)(2,1)} %all-gather.8.cloned.1.call-done, f32[]{:T(128)} %bitcast), kind=kOutput, calls=%fused_computation | convolution fusion | flops 4296015872 | bytes 12582916 | tf_op jit(solution)/shard_map/dot_general | solution.py:22
  190.6 24.5 %all-gather.4.cloned.1.call-done = bf16[4096,1024]{1,0:T(8,128)(2,1)} async-done(((bf16[1024,1024]{1,0:T(8,128)(2,1)}), bf16[4096,1024]{1,0:T(8,128)(2,1)}) %all-gather.4.cloned.1.call-update) | async-done | bytes 8388624 | tf_op jit(solution)/shard_map/all_gather | solution.py:13
  215.2 10.4 %convolution_multiply_fusion.1 = f32[1024,512]{1,0:T(8,128)} fusion(bf16[4096,1024]{1,0:T(8,128)(2,1)} %all-gather.4.cloned.1.call-done, bf16[4096,512]{1,0:T(8,128)(2,1)} %all-gather.6.cloned.1.call-done, f32[]{:T(128)} %bitcast), kind=kOutput, calls=%fused_computation.1 | convolution fusion | flops 4295491584 | bytes 14680068 | tf_op jit(solution)/shard_map/dot_general | solution.py:12
Async XLA Ops:
  7.2 85.9 %all-gather.6.cloned.1.call-start = ((), (), s32[]{:S(2)}) async-start(), calls=%async_computation.2 | async-start | bytes 5242880 | tf_op jit(solution)/shard_map/all_gather | solution.py:11
  7.9 172.7 %all-gather.8.cloned.1.call-start = ((), (), s32[]{:S(2)}) async-start(), calls=%async_computation.3 | async-start | bytes 5242880 | tf_op jit(solution)/shard_map/all_gather | solution.py:21
  8.6 206.5 %all-gather.4.cloned.1.call-start = ((), (), s32[]{:S(2)}) async-start(), calls=%async_computation.1 | async-start | bytes 10485760 | tf_op jit(solution)/shard_map/all_gather | solution.py:13
  93.0 81.2 %all-to-all-start = ((bf16[4,1024,512]{2,1,0:T(8,128)(2,1)}), bf16[4,1024,512]{2,1,0:T(8,128)(2,1)}, u32[]{:S(2)}, u32[]{:S(2)}) async-start(bf16[4,1024,512]{2,1,0:T(8,128)(2,1)} %bitcast.8), calls=%async_computation | async-start | bytes 8388608 | tf_op jit(solution)/shard_map/all_to_all | solution.py:18
Sparse Core Ops, SparseCore 0:
  9.5 83.4 all-gather.5
  94.6 55.5 all-gather.7
  151.7 63.4 all-gather.3
where the time goes:
time: 232 us
  waiting for transfers between devices  186 us (80%)
  matrix products  20.4 us (9%)
  between operations  14.4 us (6%)
  local copies, waits for them, and re-layouts  6.35 us (3%)
  starting transfers between devices  4.97 us (2%)
    all_gather x1, waiting for transfers between devices, shards(): cotangent_all = lax.all_gather(expected_cot, 'markov', axis=0, tiled=True)  83.7 us
    all_to_all x1, waiting for transfers between devices, shards(): lax.all_to_all(cotangent_all, ('storage', 'sub'), split_axis=0, concat_ax...  75.7 us
    all_gather x1, waiting for transfers between devices, shards(): lax.all_gather(transition, ('storage', 'sub'), axis=0, tiled=True)  24.5 us
    dot_general x1, matrix products, shards(): lax.dot_general(lax.all_gather(transition, ('storage', 'sub'), axis=0, ti...  10.4 us
    dot_general x1, matrix products, shards(): lax.dot_general(own_states, gathered_values, (((1,), (1,)), ((), ())), pr...  10 us
    all_to_all x1, local copies, waits for them, and re-layouts, shards(): lax.all_to_all(cotangent_all, ('storage', 'sub'), split_axis=0, concat_ax...  6.35 us
    all_to_all x1, starting transfers between devices, shards(): lax.all_to_all(cotangent_all, ('storage', 'sub'), split_axis=0, concat_ax...  4.85 us
  transfers between devices with their start and end apart: 4, of which 3 were waited for; matrix products, arithmetic and copies ran while one was open for 7% of the time, Pallas kernels for 0%

commit v1 on v0

--- a/solution.py
+++ b/solution.py
@@ -8,7 +8,23 @@
 
 def shards(expected_cot, value_next, transition, section):
     discount_factor = jnp.exp(section[0].astype(jnp.float32) * jnp.log(jnp.float32(discount_rate)))
-    cotangent_all = lax.all_gather(expected_cot, "markov", axis=0, tiled=True)
+    ways, here, step = (lax.axis_size("markov"), lax.axis_index("markov"), expected_cot.shape[0])
+    lengths = [n * ways if d == 0 else n for d, n in enumerate(expected_cot.shape)]
+    full = lax.dynamic_update_slice_in_dim(
+        jnp.zeros(lengths, expected_cot.dtype), expected_cot, here * step, axis=0
+    )
+    going_up = going_down = expected_cot
+    for far in range(1, ways // 2 + 1):
+        going_up = lax.ppermute(going_up, "markov", [(d, (d + 1) % ways) for d in range(ways)])
+        full = lax.dynamic_update_slice_in_dim(full, going_up, (here - far) % ways * step, axis=0)
+        if 2 * far < ways:
+            going_down = lax.ppermute(
+                going_down, "markov", [(d, (d - 1) % ways) for d in range(ways)]
+            )
+            full = lax.dynamic_update_slice_in_dim(
+                full, going_down, (here + far) % ways * step, axis=0
+            )
+    cotangent_all = full
     adjoint_sum = lax.dot_general(
         lax.all_gather(transition, ("storage", "sub"), axis=0, tiled=True),
         cotangent_all,

time: 232 us -> 183 us (0.79)
  waiting for transfers between devices: 186 us -> 128 us
  local copies, waits for them, and re-layouts: 6.35 us -> 12.1 us
  starting transfers between devices: 4.97 us -> 10.1 us
    all_gather x1 -> x0, waiting for transfers between devices: 83.7 us -> none  [shards(): cotangent_all = lax.all_gather(expected_cot, 'markov', axis=0, tiled=True)]
    ppermute x0 -> x3, waiting for transfers between devices: none -> 66.3 us  [the longest x2 45.5 us: shards(): lax.ppermute(going_up, 'markov', [(d, (d + 1) % ways) for d in range(ways)])]
    all_gather x1, waiting for transfers between devices: 24.5 us -> 0.01 us  [shards(): lax.all_gather(transition, ('storage', 'sub'), axis=0, tiled=True)]
    all_to_all x1, waiting for transfers between devices: 75.7 us -> 60.2 us  [shards(): lax.all_to_all(cotangent_all, ('storage', 'sub'), split_axis=0, concat_ax...]
    ppermute x0 -> x3, starting transfers between devices: none -> 5.2 us  [the longest x2 3.11 us: shards(): lax.ppermute(going_up, 'markov', [(d, (d + 1) % ways) for d in range(ways)])]
    unnamed x0 -> x5, local copies, waits for them, and re-layouts: none -> 3.73 us
  transfers between devices with their start and end apart: 4 -> 6, of which waited for: 3 -> 4; matrix products, arithmetic and copies ran while one was open for 7% -> 10% of each run, Pallas kernels for 0% -> 0%
where the time goes in v1:
time: 183 us
  waiting for transfers between devices  128 us (70%)
  matrix products  18.2 us (10%)
  between operations  14.8 us (8%)
  local copies, waits for them, and re-layouts  12.1 us (7%)
  starting transfers between devices  10.1 us (6%)
    all_to_all x1, waiting for transfers between devices, shards(): lax.all_to_all(cotangent_all, ('storage', 'sub'), split_axis=0, concat_ax...  60.2 us
    ppermute x2, waiting for transfers between devices, shards(): lax.ppermute(going_up, 'markov', [(d, (d + 1) % ways) for d in range(ways)])  45.5 us
    ppermute x1, waiting for transfers between devices, shards(): lax.ppermute(going_down, 'markov', [(d, (d - 1) % ways) for d in range(wa...  20.8 us
    dot_general x1, matrix products, shards(): lax.dot_general(own_states, gathered_values, (((1,), (1,)), ((), ())), pr...  10 us
    dot_general x1, matrix products, shards(): lax.dot_general(lax.all_gather(transition, ('storage', 'sub'), axis=0, ti...  8.22 us
    all_to_all x1, local copies, waits for them, and re-layouts, shards(): lax.all_to_all(cotangent_all, ('storage', 'sub'), split_axis=0, concat_ax...  6.35 us
    all_to_all x1, starting transfers between devices, shards(): lax.all_to_all(cotangent_all, ('storage', 'sub'), split_axis=0, concat_ax...  4.83 us
    unnamed x5, local copies, waits for them, and re-layouts  3.73 us
  transfers between devices with their start and end apart: 6, of which 4 were waited for; matrix products, arithmetic and copies ran while one was open for 10% of the time, Pallas kernels for 0%

profile of v1, /device:TPU:0, one launch (start us, length us, event | category | flops | bytes accessed | tf_op | source)
XLA Modules:
  0.0 183.1 jit_solution(16305576197843233352)
XLA Ops:
  7.2 0.0 copy-start.1
  7.2 0.0 all-gather.5.cloned.1.call-start
  7.2 0.7 all-gather.5.cloned.1.call-update
  7.9 0.0 all-gather.3.cloned.1.call-start
  8.0 0.7 all-gather.3.cloned.1.call-update
  8.7 3.1 %collective-permute-start = (bf16[1024,512]{1,0:T(8,128)(2,1)}, bf16[1024,512]{1,0:T(8,128)(2,1)S(1)}, u32[]{:S(2)}, u32[]{:S(2)}) collective-permute-start(bf16[1024,512]{1,0:T(8,128)(2,1)} %param.4), channel_id=1, source_target_pairs={{0,4},{4,8},{8,12},{12,0},{1,5},{5,9},{9,13},{13,1},{2,6},{6,10},{... | collective-permute-start | bytes 3145736 | tf_op jit(solution)/shard_map/ppermute | solution.py:18
  11.8 2.1 %collective-permute-start.1 = (bf16[1024,512]{1,0:T(8,128)(2,1)}, bf16[1024,512]{1,0:T(8,128)(2,1)}, u32[]{:S(2)}, u32[]{:S(2)}) collective-permute-start(bf16[1024,512]{1,0:T(8,128)(2,1)} %param.4), channel_id=1, source_target_pairs={{0,12},{4,0},{8,4},{12,8},{1,13},{5,1},{9,5},{13,9},{2,14},{6,2},{... | collective-permute-start | bytes 3145736 | tf_op jit(solution)/shard_map/ppermute | solution.py:21
  13.9 24.2 %collective-permute-done = bf16[1024,512]{1,0:T(8,128)(2,1)S(1)} collective-permute-done((bf16[1024,512]{1,0:T(8,128)(2,1)}, bf16[1024,512]{1,0:T(8,128)(2,1)S(1)}, u32[]{:S(2)}, u32[]{:S(2)}) %collective-permute-start) | collective-permute-done | bytes 1048608 | tf_op jit(solution)/shard_map/ppermute | solution.py:18
  38.1 0.0 collective-permute-start.2
  38.1 0.3 broadcast_in_dim.3
  38.3 0.0 copy-done.1
  38.3 0.1 constant_dynamic-update-slice_fusion.3
  38.5 0.1 constant_dynamic-update-slice_fusion.2
  38.6 20.8 %collective-permute-done.1 = bf16[1024,512]{1,0:T(8,128)(2,1)} collective-permute-done((bf16[1024,512]{1,0:T(8,128)(2,1)}, bf16[1024,512]{1,0:T(8,128)(2,1)}, u32[]{:S(2)}, u32[]{:S(2)}) %collective-permute-start.1) | collective-permute-done | bytes 1048608 | tf_op jit(solution)/shard_map/ppermute | solution.py:21
  59.4 1.4 constant_dynamic-update-slice_fusion.1
  60.8 21.3 %collective-permute-done.2 = bf16[1024,512]{1,0:T(8,128)(2,1)S(1)} collective-permute-done((bf16[1024,512]{1,0:T(8,128)(2,1)S(1)}, bf16[1024,512]{1,0:T(8,128)(2,1)S(1)}, u32[]{:S(2)}, u32[]{:S(2)}) %collective-permute-start.2) | collective-permute-done | bytes 1048608 | tf_op jit(solution)/shard_map/ppermute | solution.py:18
  82.1 0.1 constant_dynamic-update-slice_fusion
  82.3 1.9 %copy-done = bf16[4096,512]{1,0:T(8,128)(2,1)} copy-done((bf16[4096,512]{1,0:T(8,128)(2,1)}, bf16[4096,512]{1,0:T(8,128)(2,1)S(1)}, u32[]{:S(2)}) %copy-start) | copy-done | bytes 4194328
  84.2 4.8 %all-to-all-start = ((bf16[4,1024,512]{2,1,0:T(8,128)(2,1)}), bf16[4,1024,512]{2,1,0:T(8,128)(2,1)}, u32[]{:S(2)}, u32[]{:S(2)}) async-start(bf16[4,1024,512]{2,1,0:T(8,128)(2,1)} %bitcast.10), calls=%async_computation | async-start | bytes 8388608 | tf_op jit(solution)/shard_map/all_to_all | solution.py:34
  89.7 60.2 %all-to-all-done = bf16[4,1024,512]{2,1,0:T(8,128)(2,1)} async-done(((bf16[4,1024,512]{2,1,0:T(8,128)(2,1)}), bf16[4,1024,512]{2,1,0:T(8,128)(2,1)}, u32[]{:S(2)}, u32[]{:S(2)}) %all-to-all-start) | async-done | bytes 4194336 | tf_op jit(solution)/shard_map/all_to_all | solution.py:34
  149.9 6.4 %copy.8 = bf16[1024,4,512]{0,2,1:T(8,128)(2,1)} copy(bf16[1024,4,512]{2,0,1:T(8,128)(2,1)} %bitcast.3) | data formatting | bytes 8388608 | tf_op jit(solution)/shard_map/all_to_all | solution.py:34
  156.2 10.0 %convolution_multiply_fusion = f32[1024,1024]{1,0:T(8,128)} fusion(bf16[1024,2048]{0,1:T(8,128)(2,1)} %bitcast.11, bf16[1024,2048]{1,0:T(8,128)(2,1)} %all-gather.5.cloned.1.call-done, f32[]{:T(128)} %bitcast), kind=kOutput, calls=%fused_computation | convolution fusion | flops 4296015872 | bytes 12582916 | tf_op jit(solution)/shard_map/dot_general | solution.py:38
  166.2 8.2 %multiply_bitcast_fusion = f32[1024,512]{0,1:T(8,128)S(1)} fusion(bf16[4096,512]{1,0:T(8,128)(2,1)} %copy-done, bf16[4096,1024]{1,0:T(8,128)(2,1)} %all-gather.3.cloned.1.call-done, f32[]{:T(128)} %bitcast), kind=kOutput, calls=%fused_computation.1 | convolution fusion | flops 4295491584 | bytes 14680068 | tf_op jit(solution)/shard_map/dot_general | solution.py:28
  174.5 1.8 copy.9
  (3 shorter events, 0.0 us)
Async XLA Ops:
  7.2 31.2 %copy-start.1 = (bf16[1024,512]{1,0:T(8,128)(2,1)S(1)}, bf16[1024,512]{1,0:T(8,128)(2,1)}, u32[]{:S(2)}) copy-start(bf16[1024,512]{1,0:T(8,128)(2,1)} %param.4) | copy-start | bytes 3145732
  7.2 149.0 %all-gather.5.cloned.1.call-start = ((), (), s32[]{:S(2)}) async-start(), calls=%async_computation.2 | async-start | bytes 5242880 | tf_op jit(solution)/shard_map/all_gather | solution.py:37
  7.9 158.3 %all-gather.3.cloned.1.call-start = ((), (), s32[]{:S(2)}) async-start(), calls=%async_computation.1 | async-start | bytes 10485760 | tf_op jit(solution)/shard_map/all_gather | solution.py:29
  8.7 29.4 %collective-permute-start = (bf16[1024,512]{1,0:T(8,128)(2,1)}, bf16[1024,512]{1,0:T(8,128)(2,1)S(1)}, u32[]{:S(2)}, u32[]{:S(2)}) collective-permute-start(bf16[1024,512]{1,0:T(8,128)(2,1)} %param.4), channel_id=1, source_target_pairs={{0,4},{4,8},{8,12},{12,0},{1,5},{5,9},{9,13},{13,1},{2,6},{6,10},{... | collective-permute-start | bytes 3145736 | tf_op jit(solution)/shard_map/ppermute | solution.py:18
  11.8 47.6 %collective-permute-start.1 = (bf16[1024,512]{1,0:T(8,128)(2,1)}, bf16[1024,512]{1,0:T(8,128)(2,1)}, u32[]{:S(2)}, u32[]{:S(2)}) collective-permute-start(bf16[1024,512]{1,0:T(8,128)(2,1)} %param.4), channel_id=1, source_target_pairs={{0,12},{4,0},{8,4},{12,8},{1,13},{5,1},{9,5},{13,9},{2,14},{6,2},{... | collective-permute-start | bytes 3145736 | tf_op jit(solution)/shard_map/ppermute | solution.py:21
  38.1 44.1 %collective-permute-start.2 = (bf16[1024,512]{1,0:T(8,128)(2,1)S(1)}, bf16[1024,512]{1,0:T(8,128)(2,1)S(1)}, u32[]{:S(2)}, u32[]{:S(2)}) collective-permute-start(bf16[1024,512]{1,0:T(8,128)(2,1)S(1)} %collective-permute-done), channel_id=1, source_target_pairs={{0,4},{4,8},{8,12},{12,0},{1,5},{5,9},{9,13},{13,1},{2,6},{6,10},{... | collective-permute-start | bytes 3145736 | tf_op jit(solution)/shard_map/ppermute | solution.py:18
  82.2 1.9 %copy-start = (bf16[4096,512]{1,0:T(8,128)(2,1)}, bf16[4096,512]{1,0:T(8,128)(2,1)S(1)}, u32[]{:S(2)}) copy-start(bf16[4096,512]{1,0:T(8,128)(2,1)S(1)} %constant_dynamic-update-slice_fusion) | copy-start | bytes 12582916
  84.2 65.7 %all-to-all-start = ((bf16[4,1024,512]{2,1,0:T(8,128)(2,1)}), bf16[4,1024,512]{2,1,0:T(8,128)(2,1)}, u32[]{:S(2)}, u32[]{:S(2)}) async-start(bf16[4,1024,512]{2,1,0:T(8,128)(2,1)} %bitcast.10), calls=%async_computation | async-start | bytes 8388608 | tf_op jit(solution)/shard_map/all_to_all | solution.py:34
Sparse Core Ops, SparseCore 0:
  9.5 37.1 all-gather.4
  48.3 70.9 all-gather.2

commit v2 on v0

--- a/solution.py
+++ b/solution.py
@@ -10,7 +10,15 @@
     discount_factor = jnp.exp(section[0].astype(jnp.float32) * jnp.log(jnp.float32(discount_rate)))
     cotangent_all = lax.all_gather(expected_cot, "markov", axis=0, tiled=True)
     adjoint_sum = lax.dot_general(
-        lax.all_gather(transition, ("storage", "sub"), axis=0, tiled=True),
+        jnp.concatenate(
+            lax.all_to_all(
+                jnp.stack([transition] * lax.axis_size(("storage", "sub"))),
+                ("storage", "sub"),
+                0,
+                0,
+            ),
+            axis=0,
+        ),
         cotangent_all,
         (((0,), (0,)), ((), ())),
         preferred_element_type=jnp.float32,

time: 232 us -> 204 us (0.88)
  waiting for transfers between devices: 186 us -> 146 us
  local copies, waits for them, and re-layouts: 6.35 us -> 12.3 us
  starting transfers between devices: 4.97 us -> 10.6 us
    all_to_all x0 -> x1, waiting for transfers between devices: none -> 104 us  [shards(): lax.all_to_all(jnp.stack([transition] * lax.axis_size(('storage', 'sub'))...]
    all_gather x1, waiting for transfers between devices: 83.7 us -> 0.01 us  [shards(): cotangent_all = lax.all_gather(expected_cot, 'markov', axis=0, tiled=True)]
    all_to_all x1, waiting for transfers between devices: 75.7 us -> 40.8 us  [shards(): lax.all_to_all(cotangent_all, ('storage', 'sub'), split_axis=0, concat_ax...]
    all_gather x1 -> x0, waiting for transfers between devices: 24.5 us -> none  [shards(): lax.all_gather(transition, ('storage', 'sub'), axis=0, tiled=True)]
    another operation x0 -> x1, local copies, waits for them, and re-layouts: none -> 6.02 us  [shards(): jnp.stack([transition] * lax.axis_size(('storage', 'sub')))]
    all_to_all x0 -> x1, starting transfers between devices: none -> 5.64 us  [shards(): lax.all_to_all(jnp.stack([transition] * lax.axis_size(('storage', 'sub'))...]
  transfers between devices with their start and end apart: 4 -> 4, of which waited for: 3 -> 2; matrix products, arithmetic and copies ran while one was open for 7% -> 11% of each run, Pallas kernels for 0% -> 0%
where the time goes in v2:
time: 204 us
  waiting for transfers between devices  146 us (72%)
  matrix products  20.5 us (10%)
  between operations  14.7 us (7%)
  local copies, waits for them, and re-layouts  12.3 us (6%)
  starting transfers between devices  10.6 us (5%)
    all_to_all x1, waiting for transfers between devices, shards(): lax.all_to_all(jnp.stack([transition] * lax.axis_size(('storage', 'sub'))...  104 us
    all_to_all x1, waiting for transfers between devices, shards(): lax.all_to_all(cotangent_all, ('storage', 'sub'), split_axis=0, concat_ax...  40.8 us
    dot_general x1, matrix products, shards(): lax.dot_general(jnp.concatenate(lax.all_to_all(jnp.stack([transition] * l...  10.5 us
    dot_general x1, matrix products, shards(): lax.dot_general(own_states, gathered_values, (((1,), (1,)), ((), ())), pr...  10 us
    all_to_all x1, local copies, waits for them, and re-layouts, shards(): lax.all_to_all(cotangent_all, ('storage', 'sub'), split_axis=0, concat_ax...  6.3 us
    another operation x1, local copies, waits for them, and re-layouts, shards(): jnp.stack([transition] * lax.axis_size(('storage', 'sub')))  6.02 us
    all_to_all x1, starting transfers between devices, shards(): lax.all_to_all(jnp.stack([transition] * lax.axis_size(('storage', 'sub'))...  5.64 us
    all_to_all x1, starting transfers between devices, shards(): lax.all_to_all(cotangent_all, ('storage', 'sub'), split_axis=0, concat_ax...  4.92 us
  transfers between devices with their start and end apart: 4, of which 2 were waited for; matrix products, arithmetic and copies ran while one was open for 11% of the time, Pallas kernels for 0%

profile of v2, /device:TPU:0, one launch (start us, length us, event | category | flops | bytes accessed | tf_op | source)
XLA Modules:
  0.0 204.0 jit_solution(6479692169010101072)
XLA Ops:
  7.2 0.0 all-gather.3.cloned.1.call-start
  7.2 0.7 all-gather.3.cloned.1.call-update
  7.9 6.0 %stack.2 = bf16[4,1024,1024]{2,1,0:T(8,128)(2,1)} broadcast(bf16[1024,1024]{1,0:T(8,128)(2,1)} %param.6), dimensions={1,2} | broadcast | bytes 10485760 | tf_op jit(solution)/shard_map/stack | solution.py:15
  13.9 5.6 %all-to-all-start = ((bf16[4,1024,1024]{2,1,0:T(8,128)(2,1)}), bf16[4,1024,1024]{2,1,0:T(8,128)(2,1)}, u32[]{:S(2)}, u32[]{:S(2)}) async-start(bf16[4,1024,1024]{2,1,0:T(8,128)(2,1)} %stack.2), calls=%async_computation | async-start | bytes 16777216 | tf_op jit(solution)/shard_map/all_to_all | solution.py:14
  19.6 0.0 all-gather.5.cloned.1.call-start
  19.6 0.7 all-gather.5.cloned.1.call-update
  20.3 103.6 %all-to-all-done = bf16[4,1024,1024]{2,1,0:T(8,128)(2,1)} async-done(((bf16[4,1024,1024]{2,1,0:T(8,128)(2,1)}), bf16[4,1024,1024]{2,1,0:T(8,128)(2,1)}, u32[]{:S(2)}, u32[]{:S(2)}) %all-to-all-start) | async-done | bytes 8388640 | tf_op jit(solution)/shard_map/all_to_all | solution.py:14
  124.0 0.0 all-gather.3.cloned.1.call-done
  124.0 4.9 %all-to-all-start.1 = ((bf16[4,1024,512]{2,1,0:T(8,128)(2,1)}), bf16[4,1024,512]{2,1,0:T(8,128)(2,1)}, u32[]{:S(2)}, u32[]{:S(2)}) async-start(bf16[4,1024,512]{2,1,0:T(8,128)(2,1)} %bitcast.9), calls=%async_computation.1 | async-start | bytes 8388608 | tf_op jit(solution)/shard_map/all_to_all | solution.py:26
  129.6 10.5 %convolution_multiply_fusion.1 = f32[1024,512]{1,0:T(8,128)} fusion(bf16[4096,1024]{1,0:T(8,128)(2,1)} %bitcast.1, bf16[4096,512]{1,0:T(8,128)(2,1)} %all-gather.3.cloned.1.call-done, f32[]{:T(128)} %bitcast), kind=kOutput, calls=%fused_computation.1 | convolution fusion | flops 4295491584 | bytes 14680068 | tf_op jit(solution)/shard_map/dot_general | solution.py:12
  140.0 40.8 %all-to-all-done.1 = bf16[4,1024,512]{2,1,0:T(8,128)(2,1)} async-done(((bf16[4,1024,512]{2,1,0:T(8,128)(2,1)}), bf16[4,1024,512]{2,1,0:T(8,128)(2,1)}, u32[]{:S(2)}, u32[]{:S(2)}) %all-to-all-start.1) | async-done | bytes 4194336 | tf_op jit(solution)/shard_map/all_to_all | solution.py:26
  180.8 6.3 %copy.6 = bf16[1024,4,512]{0,2,1:T(8,128)(2,1)} copy(bf16[1024,4,512]{2,0,1:T(8,128)(2,1)} %bitcast.3) | data formatting | bytes 8388608 | tf_op jit(solution)/shard_map/all_to_all | solution.py:26
  187.1 0.0 all-gather.5.cloned.1.call-done
  187.1 10.0 %convolution_multiply_fusion = f32[1024,1024]{1,0:T(8,128)} fusion(bf16[1024,2048]{0,1:T(8,128)(2,1)} %bitcast.10, bf16[1024,2048]{1,0:T(8,128)(2,1)} %all-gather.5.cloned.1.call-done, f32[]{:T(128)} %bitcast), kind=kOutput, calls=%fused_computation | convolution fusion | flops 4296015872 | bytes 12582916 | tf_op jit(solution)/shard_map/dot_general | solution.py:30
Async XLA Ops:
  7.2 116.8 %all-gather.3.cloned.1.call-start = ((), (), s32[]{:S(2)}) async-start(), calls=%async_computation.2 | async-start | bytes 5242880 | tf_op jit(solution)/shard_map/all_gather | solution.py:11
  13.9 110.0 %all-to-all-start = ((bf16[4,1024,1024]{2,1,0:T(8,128)(2,1)}), bf16[4,1024,1024]{2,1,0:T(8,128)(2,1)}, u32[]{:S(2)}, u32[]{:S(2)}) async-start(bf16[4,1024,1024]{2,1,0:T(8,128)(2,1)} %stack.2), calls=%async_computation | async-start | bytes 16777216 | tf_op jit(solution)/shard_map/all_to_all | solution.py:14
  19.6 167.5 %all-gather.5.cloned.1.call-start = ((), (), s32[]{:S(2)}) async-start(), calls=%async_computation.3 | async-start | bytes 5242880 | tf_op jit(solution)/shard_map/all_gather | solution.py:29
  124.0 56.8 %all-to-all-start.1 = ((bf16[4,1024,512]{2,1,0:T(8,128)(2,1)}), bf16[4,1024,512]{2,1,0:T(8,128)(2,1)}, u32[]{:S(2)}, u32[]{:S(2)}) async-start(bf16[4,1024,512]{2,1,0:T(8,128)(2,1)} %bitcast.9), calls=%async_computation.1 | async-start | bytes 8388608 | tf_op jit(solution)/shard_map/all_to_all | solution.py:26
Sparse Core Ops, SparseCore 0:
  9.5 83.4 all-gather.2
  94.6 46.1 all-gather.4
